TPU v7x, 128 devices: a whole 4x4x4 slice. The times are simulated.
128 devices in a mesh: blk: 16 (over y_lo, x, core), mp: 8 (over z, y_hi).
Axes of the slice: x: 4, y: 4 (y_hi: 2, y_lo: 2; y = y_hi * 2 + y_lo), z: 4, core: 2. Of those that a mesh axis runs over, the one named last changes fastest.
Arguments:
- features: bfloat16 [32768, 768], P('blk', 'mp'), may hold values from -9 to 9
- edge_dst: int32 [1024], P('blk'), may hold values from 0 to 15
- edge_src: int32 [1024], P('blk'), may hold values from 0 to 255
- edge_mask: int32 [1024, 128, 128], P('blk'), may hold values 0 or 1
- gin_in: bfloat16 [768, 768], P(None, 'mp'), may hold values from -0.21875 to 0.21875
- gin_out: bfloat16 [768, 768], P('mp'), may hold values from -0.21875 to 0.21875
- w_query: bfloat16 [768, 512], P(None, 'mp'), may hold values from -1 to 1
- w_key: bfloat16 [768, 512], P(None, 'mp'), may hold values from -1 to 1
- w_value: bfloat16 [768, 512], P(None, 'mp'), may hold values from -0.21875 to 0.21875
- w_attn_out: bfloat16 [512, 768], P('mp'), may hold values from -4 to 4
- ffn_in: bfloat16 [768, 1536], P(None, 'mp'), may hold values from -0.21875 to 0.21875
- ffn_out: bfloat16 [1536, 768], P('mp'), may hold values from -0.15625 to 0.15625
Outputs:
- layer_out: bfloat16 [32768, 768], P('blk', 'mp')
Inputs may be any that keep to these rules, and one draw needn't show every extreme that they name: `edge_dst`: local destination block of an edge block. `edge_src`: source block over the whole batch; several edge blocks may share a pair.
All inputs are finite; a program needn't handle non-finite values. No bound on the sum of `edge_mask` on one device may be relied on, other than what follows from the above.
Results may differ from a plain program's by a relative error of at most 0.011.
Values may be sent and summed in bfloat16 or wider, within the bound.
A program may use at most 128 MiB of HBM per device.

v0:
```python
import math
import jax
import jax.numpy as jnp
from jax import lax
from jax.sharding import PartitionSpec as P

HEAD_DIM = 64
BLOCK = 128


def neighbour_parts(features, edge_dst, edge_src, edge_mask):
    rows, cols = features.shape
    local_blocks = rows // BLOCK
    edge_count = edge_src.shape[0]

    def collect(pulled_all, piece, start):
        count = piece.shape[0] // BLOCK
        blocks = piece.reshape(count, BLOCK, cols)
        inside = jnp.logical_and(edge_src >= 0, edge_src < count)
        pulled = jnp.take(blocks, jnp.clip(edge_src, 0, count - 1), axis=0)
        return jnp.where(inside[:, None, None], pulled, pulled_all)

    def neighbour_finish(pulled_all):
        summand_terms = jnp.einsum(
            "ers,esf->erf",
            edge_mask.astype(jnp.bfloat16),
            pulled_all,
            preferred_element_type=jnp.float32,
        )
        target_nodes = (
            edge_dst[:, None] == jnp.arange(local_blocks, dtype=jnp.int32)[None, :]
        ).astype(jnp.float32)
        running_total = jnp.einsum(
            "cy,cla->yla", target_nodes, summand_terms, precision=lax.Precision.HIGHEST
        )
        return running_total.reshape(rows, cols)

    empty = jnp.zeros((edge_count, BLOCK, cols), features.dtype)
    return (collect, neighbour_finish, empty)


def attention_parts(whole, w_query, w_key, w_value):
    rows = whole.shape[0]
    heads = w_query.shape[1] // HEAD_DIM
    scale = 1.0 / math.sqrt(HEAD_DIM)
    queries = jnp.dot(whole, w_query, preferred_element_type=jnp.float32).astype(jnp.bfloat16)
    keys = jnp.dot(whole, w_key, preferred_element_type=jnp.float32).astype(jnp.bfloat16)
    values = jnp.dot(whole, w_value, preferred_element_type=jnp.float32).astype(jnp.bfloat16)
    query_heads = queries.reshape(rows, heads, HEAD_DIM)

    def add_keys(state, pieces, start):
        key_row_matrix, value_rows = pieces
        count = key_row_matrix.shape[0] // rows
        key_blocks = key_row_matrix.reshape(count, rows, heads, HEAD_DIM)
        value_blocks = value_rows.reshape(count, rows, heads, HEAD_DIM)

        def one_block(carry, operands):
            best, running_total, summed = carry
            key_block, value_block = operands
            scores = (
                jnp.einsum(
                    "qhd,khd->hqk", query_heads, key_block, preferred_element_type=jnp.float32
                )
                * scale
            )
            newest = jnp.maximum(best, jnp.max(scores, axis=-1))
            fade = jnp.exp(best - newest)
            expo = jnp.exp(scores - newest[..., None])
            running_total = running_total * fade + jnp.sum(expo, axis=-1)
            summed = summed * fade[..., None] + jnp.einsum(
                "hqk,khd->hqd",
                expo.astype(jnp.bfloat16),
                value_block,
                preferred_element_type=jnp.float32,
            )
            return ((newest, running_total, summed), None)

        state, _ = lax.scan(one_block, state, (key_blocks, value_blocks))
        return state

    def attention_finish(state):
        best, running_total, summed = state
        attended = (summed / running_total[..., None]).astype(jnp.bfloat16)
        return attended.transpose(1, 0, 2).reshape(rows, heads * HEAD_DIM)

    start_state = (
        jnp.full((heads, rows), -1e30, jnp.float32),
        jnp.zeros((heads, rows), jnp.float32),
        jnp.zeros((heads, rows, HEAD_DIM), jnp.float32),
    )
    return (add_keys, attention_finish, start_state, keys, values)


def per_device(
    features,
    edge_dst,
    edge_src,
    edge_mask,
    gin_in,
    gin_out,
    w_query,
    w_key,
    w_value,
    w_attn_out,
    ffn_in,
    ffn_out,
):
    rows, cols = features.shape
    width = cols * lax.axis_size("mp")
    whole = lax.all_gather(features, "mp", axis=1, tiled=True)
    collect, completed_rows, empty = neighbour_parts(features, edge_dst, edge_src, edge_mask)
    add_keys, finish_keys, start_state, keys, values = attention_parts(
        whole, w_query, w_key, w_value
    )
    pulled_all = collect(empty, lax.all_gather(features, "blk", axis=0, tiled=True), jnp.int32(0))
    state = add_keys(
        start_state,
        (
            lax.all_gather(keys, "blk", axis=0, tiled=True),
            lax.all_gather(values, "blk", axis=0, tiled=True),
        ),
        jnp.int32(0),
    )
    gathered = completed_rows(pulled_all)
    attended = finish_keys(state)
    local_share = (features.astype(jnp.float32) + gathered * 0.25).astype(jnp.bfloat16)
    local_in = lax.all_gather(local_share, "mp", axis=1, tiled=True)
    local_hidden = jax.nn.relu(
        jnp.dot(local_in, gin_in, preferred_element_type=jnp.float32)
    ).astype(jnp.bfloat16)
    partial_sum = jnp.dot(local_hidden, gin_out, preferred_element_type=jnp.float32) + jnp.dot(
        attended, w_attn_out, preferred_element_type=jnp.float32
    )
    mixed = lax.psum(partial_sum, "mp") + whole.astype(jnp.float32)
    row_average = jnp.sum(mixed, axis=1, keepdims=True) / width
    square_row = jnp.sum(mixed * mixed, axis=1, keepdims=True) / width
    normed = (
        (mixed - row_average) * lax.rsqrt(square_row - row_average * row_average + 1e-05)
    ).astype(jnp.bfloat16)
    mixed_share = lax.dynamic_slice_in_dim(mixed, lax.axis_index("mp") * cols, cols, 1)
    ffn_hidden = jax.nn.relu(jnp.dot(normed, ffn_in, preferred_element_type=jnp.float32)).astype(
        jnp.bfloat16
    )
    ffn_terms = jnp.dot(ffn_hidden, ffn_out, preferred_element_type=jnp.float32)
    return (
        mixed_share + lax.psum_scatter(ffn_terms, "mp", scatter_dimension=1, tiled=True)
    ).astype(jnp.bfloat16)


def solution(mesh):
    return jax.shard_map(
        per_device,
        mesh=mesh,
        in_specs=(
            P("blk", "mp"),
            P("blk"),
            P("blk"),
            P("blk", None, None),
            P(None, "mp"),
            P("mp", None),
            P(None, "mp"),
            P(None, "mp"),
            P(None, "mp"),
            P("mp", None),
            P(None, "mp"),
            P("mp", None),
        ),
        out_specs=P("blk", "mp"),
        check_vma=False,
    )
```

profile of v0, /device:TPU:1, one launch (start us, length us, event | category | flops | bytes accessed | tf_op | source)
XLA Modules:
  0.0 1045.0 jit_solution(14462335083314807584)
XLA Ops:
  8.1 67.3 %all-gather.10.cloned.1.call-done = bf16[2048,768]{0,1:T(8,128)(2,1)} async-done(((bf16[2048,96]{0,1:T(8,128)(2,1)}), bf16[2048,768]{0,1:T(8,128)(2,1)}) %all-gather.10.cloned.1.call-update) | async-done | bytes 3145744 | tf_op jit(solution)/shard_map/all_gather | solution.py:110
  82.7 35.2 %all-gather.6.cloned.1.call-done = bf16[32768,96]{0,1:T(8,128)(2,1)} async-done(((bf16[2048,96]{0,1:T(8,128)(2,1)}), bf16[32768,96]{0,1:T(8,128)(2,1)}) %all-gather.6.cloned.1.call-update) | async-done | bytes 6291472 | tf_op jit(solution)/shard_map/all_gather | solution.py:115
  137.6 20.1 %all-gather.12.cloned.1.call-done = bf16[32768,64]{0,1:T(8,128)(2,1)} async-done(((bf16[2048,64]{0,1:T(8,128)(2,1)}), bf16[32768,64]{0,1:T(8,128)(2,1)}) %all-gather.12.cloned.1.call-update) | async-done | bytes 4194320 | tf_op jit(solution)/shard_map/all_gather | solution.py:119
  166.6 30.1 %all-gather.14.cloned.1.call-done = bf16[32768,64]{0,1:T(8,128)(2,1)} async-done(((bf16[2048,64]{0,1:T(8,128)(2,1)}), bf16[32768,64]{0,1:T(8,128)(2,1)}) %all-gather.14.cloned.1.call-update) | async-done | bytes 4194320 | tf_op jit(solution)/shard_map/all_gather | solution.py:120
  205.5 440.0 %while.15 = (s32[]{:T(128)}, f32[1,2048]{1,0:T(1,128)S(1)}, f32[1,2048]{1,0:T(1,128)S(1)}, f32[1,2048,64]{1,2,0:T(8,128)}, bf16[16,2048,1,64]{1,3,2,0:T(8,128)(2...) while((s32[]{:T(128)}, f32[1,2048]{1,0:T(1,128)S(1)}, ...), condition=%wide.region_3.4_spmd.clone, body=%wide.region_0.0_spmd.clone.sunk | while | flops 1107699712 | bytes 52298852 | solution.py:78
  205.5 9.2 multiply_reduce_fusion.3
  223.4 9.6 fusion.82
  233.0 9.2 multiply_reduce_fusion.3
  250.8 9.8 fusion.82
  260.7 9.2 multiply_reduce_fusion.3
  278.5 9.7 fusion.82
  288.1 9.2 multiply_reduce_fusion.3
  306.0 9.7 fusion.82
  315.6 9.2 multiply_reduce_fusion.3
  333.4 9.7 fusion.82
  360.9 9.7 fusion.82
  370.6 9.2 multiply_reduce_fusion.3
  388.4 9.7 fusion.82
  398.1 9.2 multiply_reduce_fusion.3
  415.9 9.7 fusion.82
  425.6 9.2 multiply_reduce_fusion.3
  443.4 9.7 fusion.82
  453.1 9.2 multiply_reduce_fusion.3
  470.9 9.7 fusion.82
  498.4 9.7 fusion.82
  525.8 9.7 fusion.82
  553.3 9.7 fusion.82
  580.8 9.7 fusion.82
  608.3 9.7 fusion.82
  635.8 9.7 fusion.82
  661.4 259.9 %all-reduce.2.cloned.1.call-done = f32[2048,768]{1,0:T(8,128)} async-done(((f32[2048,768]{1,0:T(8,128)}), f32[2048,768]{1,0:T(8,128)}) %all-reduce.2.cloned.1.call-update) | async-done | bytes 6291472 | tf_op jit(solution)/shard_map/psum | solution.py:134
  936.0 97.9 %reduce-scatter.4.cloned.1.call-done = f32[96,2048]{1,0:T(8,128)} async-done(((f32[768,2048]{1,0:T(8,128)}), f32[96,2048]{1,0:T(8,128)}) %reduce-scatter.4.cloned.1.call-update) | async-done | bytes 786448
  (126 shorter events, 283.2 us)
Async XLA Ops:
  6.5 921.8 %copy-start = (bf16[192,768]{1,0:T(8,128)(2,1)S(1)}, bf16[192,768]{1,0:T(8,128)(2,1)}, u32[]{:S(2)}) copy-start(bf16[192,768]{1,0:T(8,128)(2,1)} %param.25) | copy-start | bytes 884740
  6.5 72.4 %copy-start.4 = (bf16[768,64]{0,1:T(8,128)(2,1)S(1)}, bf16[768,64]{0,1:T(8,128)(2,1)}, u32[]{:S(2)}) copy-start(bf16[768,64]{0,1:T(8,128)(2,1)} %param.22) | copy-start | bytes 294916
  6.5 73.9 %copy-start.6 = (s32[64]{0:T(128)S(1)}, s32[64]{0:T(128)}, u32[]{:S(2)}) copy-start(s32[64]{0:T(128)} %param.16) | copy-start | bytes 772
  6.5 68.8 %all-gather.10.cloned.1.call-start = ((), (), s32[]{:S(2)}) async-start(), calls=%async_computation.3 | async-start | bytes 3538944 | tf_op jit(solution)/shard_map/all_gather | solution.py:110
  7.3 110.6 %all-gather.6.cloned.1.call-start = ((), (), s32[]{:S(2)}) async-start(), calls=%async_computation.1 | async-start | bytes 6684672 | tf_op jit(solution)/shard_map/all_gather | solution.py:115
  8.0 149.7 %all-gather.12.cloned.1.call-start = ((), (), s32[]{:S(2)}) async-start(), calls=%async_computation.4 | async-start | bytes 4456448 | tf_op jit(solution)/shard_map/all_gather | solution.py:119
  75.4 3.5 copy-start.1
  78.8 117.8 %all-gather.14.cloned.1.call-start = ((), (), s32[]{:S(2)}) async-start(), calls=%async_computation.5 | async-start | bytes 4456448 | tf_op jit(solution)/shard_map/all_gather | solution.py:120
  80.3 565.1 %all-gather.8.cloned.1.call-start = ((), (), s32[]{:S(2)}) async-start(), calls=%async_computation.2 | async-start | bytes 3538944 | tf_op jit(solution)/shard_map/all_gather | solution.py:127
  129.1 4.3 copy-start.5
  133.4 2.9 copy-start.2
  137.4 784.0 %all-reduce.2.cloned.1.call-start = ((), (), s32[]{:S(2)}) async-start(), calls=%async_computation.6 | async-start | bytes 12582912 | tf_op jit(solution)/shard_map/psum | solution.py:134
  658.3 375.6 %reduce-scatter.4.cloned.1.call-start = ((), (), s32[]{:S(2)}) async-start(), calls=%async_computation.7 | async-start | bytes 7077888
  661.4 266.9 %copy-start.3 = (bf16[768,192]{0,1:T(8,128)(2,1)S(1)}, bf16[768,192]{0,1:T(8,128)(2,1)}, u32[]{:S(2)}) copy-start(bf16[768,192]{0,1:T(8,128)(2,1)} %param.24) | copy-start | bytes 884740
Sparse Core Ops, SparseCore 0:
  9.7 65.6 all-gather.9
  77.0 40.8 all-gather.5
  119.5 38.1 all-gather.11
  159.2 37.3 all-gather.13
  198.8 62.1 all-gather.7
  658.4 262.9 all-reduce.1
  936.1 97.7 reduce-scatter.3
where the time goes:
time: 1050 us
  waiting for transfers between devices  512 us (49%)
  matrix products  337 us (32%)
  other arithmetic  148 us (14%)
  local copies, waits for them, and re-layouts  34.5 us (3%)
  between operations  13.6 us (1%)
    psum x1, waiting for transfers between devices, per_device(): mixed = lax.psum(partial_sum, 'mp') + whole.astype(jnp.float32)  260 us
    dot_general x16, matrix products, one_block(): jnp.einsum('hqk,khd->hqd', expo.astype(jnp.bfloat16), value_block, prefer...  155 us
    dot_general x16, matrix products, one_block(): jnp.einsum('qhd,khd->hqk', query_heads, key_block, preferred_element_type...  147 us
    reduce_sum x16, other arithmetic, one_block(): running_total = running_total * fade + jnp.sum(expo, axis=-1)  137 us
    unnamed x8, waiting for transfers between devices  99.4 us
    all_gather x1, waiting for transfers between devices, per_device(): whole = lax.all_gather(features, 'mp', axis=1, tiled=True)  67.3 us
    all_gather x1, waiting for transfers between devices, per_device(): lax.all_gather(features, 'blk', axis=0, tiled=True)  35.2 us
    all_gather x1, waiting for transfers between devices, per_device(): lax.all_gather(values, 'blk', axis=0, tiled=True)  30.1 us
  transfers between devices with their start and end apart: 7, of which 6 were waited for; matrix products, arithmetic and copies ran while one was open for 47% of the time, Pallas kernels for 0%

commit v1 on v0

--- a/solution.py
+++ b/solution.py
@@ -131,7 +131,7 @@
     partial_sum = jnp.dot(local_hidden, gin_out, preferred_element_type=jnp.float32) + jnp.dot(
         attended, w_attn_out, preferred_element_type=jnp.float32
     )
-    mixed = lax.psum(partial_sum, "mp") + whole.astype(jnp.float32)
+    mixed = jnp.sum(lax.all_gather(partial_sum, "mp"), axis=0) + whole.astype(jnp.float32)
     row_average = jnp.sum(mixed, axis=1, keepdims=True) / width
     square_row = jnp.sum(mixed * mixed, axis=1, keepdims=True) / width
     normed = (

time: 1050 us -> 1290 us (1.23)
  waiting for transfers between devices: 512 us -> 736 us
  other arithmetic: 148 us -> 169 us
    all_gather x0 -> x1, waiting for transfers between devices: none -> 485 us  [per_device(): lax.all_gather(partial_sum, 'mp')]
    psum x1 -> x0, waiting for transfers between devices: 260 us -> none  [per_device(): mixed = lax.psum(partial_sum, 'mp') + whole.astype(jnp.float32)]
    unnamed x8 -> x7, waiting for transfers between devices: 99.4 us -> 1.49 us
    reduce_scatter x0 -> x1, waiting for transfers between devices: none -> 96.3 us  [per_device(): lax.psum_scatter(ffn_terms, 'mp', scatter_dimension=1, tiled=True)]
    reduce_sum x0 -> x1, other arithmetic: none -> 21.1 us  [per_device(): jnp.sum(lax.all_gather(partial_sum, 'mp'), axis=0)]
  transfers between devices with their start and end apart: 7 -> 7, of which waited for: 6 -> 6; matrix products, arithmetic and copies ran while one was open for 47% -> 37% of each run, Pallas kernels for 0% -> 0%
where the time goes in v1:
time: 1290 us
  waiting for transfers between devices  736 us (57%)
  matrix products  335 us (26%)
  other arithmetic  169 us (13%)
  local copies, waits for them, and re-layouts  35.5 us (3%)
  between operations  13.6 us (1%)
    all_gather x1, waiting for transfers between devices, per_device(): lax.all_gather(partial_sum, 'mp')  485 us
    dot_general x16, matrix products, one_block(): jnp.einsum('hqk,khd->hqd', expo.astype(jnp.bfloat16), value_block, prefer...  155 us
    dot_general x16, matrix products, one_block(): jnp.einsum('qhd,khd->hqk', query_heads, key_block, preferred_element_type...  146 us
    reduce_sum x16, other arithmetic, one_block(): running_total = running_total * fade + jnp.sum(expo, axis=-1)  137 us
    reduce_scatter x1, waiting for transfers between devices, per_device(): lax.psum_scatter(ffn_terms, 'mp', scatter_dimension=1, tiled=True)  96.3 us
    all_gather x1, waiting for transfers between devices, per_device(): whole = lax.all_gather(features, 'mp', axis=1, tiled=True)  67.3 us
    all_gather x1, waiting for transfers between devices, per_device(): lax.all_gather(features, 'blk', axis=0, tiled=True)  35.2 us
    all_gather x1, waiting for transfers between devices, per_device(): lax.all_gather(values, 'blk', axis=0, tiled=True)  30.1 us
  transfers between devices with their start and end apart: 7, of which 6 were waited for; matrix products, arithmetic and copies ran while one was open for 37% of the time, Pallas kernels for 0%

profile of v1, /device:TPU:1, one launch (start us, length us, event | category | flops | bytes accessed | tf_op | source)
XLA Modules:
  0.0 1290.0 jit_solution(3874442527426745642)
XLA Ops:
  8.1 67.3 %all-gather.12.cloned.1.call-done = bf16[2048,768]{0,1:T(8,128)(2,1)} async-done(((bf16[2048,96]{0,1:T(8,128)(2,1)}), bf16[2048,768]{0,1:T(8,128)(2,1)}) %all-gather.12.cloned.1.call-update) | async-done | bytes 3145744 | tf_op jit(solution)/shard_map/all_gather | solution.py:110
  82.7 35.2 %all-gather.8.cloned.1.call-done = bf16[32768,96]{0,1:T(8,128)(2,1)} async-done(((bf16[2048,96]{0,1:T(8,128)(2,1)}), bf16[32768,96]{0,1:T(8,128)(2,1)}) %all-gather.8.cloned.1.call-update) | async-done | bytes 6291472 | tf_op jit(solution)/shard_map/all_gather | solution.py:115
  137.6 20.1 %all-gather.14.cloned.1.call-done = bf16[32768,64]{0,1:T(8,128)(2,1)} async-done(((bf16[2048,64]{0,1:T(8,128)(2,1)}), bf16[32768,64]{0,1:T(8,128)(2,1)}) %all-gather.14.cloned.1.call-update) | async-done | bytes 4194320 | tf_op jit(solution)/shard_map/all_gather | solution.py:119
  166.5 30.1 %all-gather.16.cloned.1.call-done = bf16[32768,64]{0,1:T(8,128)(2,1)} async-done(((bf16[2048,64]{0,1:T(8,128)(2,1)}), bf16[32768,64]{0,1:T(8,128)(2,1)}) %all-gather.16.cloned.1.call-update) | async-done | bytes 4194320 | tf_op jit(solution)/shard_map/all_gather | solution.py:120
  205.5 439.0 %while.15 = (s32[]{:T(128)}, f32[1,2048]{1,0:T(1,128)S(1)}, f32[1,2048]{1,0:T(1,128)S(1)}, f32[1,2048,64]{1,2,0:T(8,128)}, bf16[16,2048,1,64]{1,3,2,0:T(8,128)(2...) while((s32[]{:T(128)}, f32[1,2048]{1,0:T(1,128)S(1)}, ...), condition=%wide.region_3.4_spmd.clone, body=%wide.region_0.0_spmd.clone.sunk | while | flops 1107699712 | bytes 52298852 | solution.py:78
  205.5 9.1 multiply_reduce_fusion.3
  223.3 9.6 fusion.83
  250.7 9.8 fusion.83
  260.5 9.1 multiply_reduce_fusion.3
  278.3 9.7 fusion.83
  305.7 9.7 fusion.83
  315.4 9.1 multiply_reduce_fusion.3
  333.1 9.7 fusion.83
  360.6 9.7 fusion.83
  370.3 9.1 multiply_reduce_fusion.3
  388.0 9.7 fusion.83
  415.4 9.7 fusion.83
  425.1 9.1 multiply_reduce_fusion.3
  442.9 9.7 fusion.83
  470.3 9.7 fusion.83
  480.0 9.1 multiply_reduce_fusion.3
  497.7 9.7 fusion.83
  525.1 9.7 fusion.83
  534.8 9.1 multiply_reduce_fusion.3
  552.6 9.7 fusion.83
  580.0 9.7 fusion.83
  589.7 9.1 multiply_reduce_fusion.3
  607.4 9.7 fusion.83
  634.8 9.7 fusion.83
  657.3 485.3 %all-gather.18.cloned.1.call-done = f32[16384,768]{1,0:T(8,128)} async-done(((f32[2048,768]{1,0:T(8,128)}), f32[16384,768]{1,0:T(8,128)}) %all-gather.18.cloned.1.call-update) | async-done | bytes 50331664 | tf_op jit(solution)/shard_map/all_gather | solution.py:134
  1142.6 21.1 %reduce_sum.38 = f32[2048,768]{1,0:T(8,128)} reduce(f32[8,2048,768]{2,1,0:T(8,128)} %bitcast.83, f32[]{:T(128)} %constant.31.clone.1), dimensions={0}, to_apply=%region_4.5 | reduce | flops 11010048 | bytes 56623108 | tf_op jit(solution)/shard_map/reduce_sum | solution.py:134
  1184.6 96.3 %reduce-scatter.2.cloned.1.call-done = f32[2048,96]{0,1:T(8,128)} async-done(((f32[2048,768]{0,1:T(8,128)}), f32[2048,96]{0,1:T(8,128)}) %reduce-scatter.2.cloned.1.call-update) | async-done | bytes 786448 | tf_op jit(solution)/shard_map/reduce_scatter | solution.py:146
  (123 shorter events, 292.8 us)
Async XLA Ops:
  6.5 1170.9 %copy-start = (bf16[192,768]{1,0:T(8,128)(2,1)S(1)}, bf16[192,768]{1,0:T(8,128)(2,1)}, u32[]{:S(2)}) copy-start(bf16[192,768]{1,0:T(8,128)(2,1)} %param.25) | copy-start | bytes 884740
  6.5 72.4 %copy-start.3 = (bf16[768,64]{0,1:T(8,128)(2,1)S(1)}, bf16[768,64]{0,1:T(8,128)(2,1)}, u32[]{:S(2)}) copy-start(bf16[768,64]{0,1:T(8,128)(2,1)} %param.22) | copy-start | bytes 294916
  6.5 73.9 %copy-start.5 = (s32[64]{0:T(128)S(1)}, s32[64]{0:T(128)}, u32[]{:S(2)}) copy-start(s32[64]{0:T(128)} %param.16) | copy-start | bytes 772
  6.5 68.8 %all-gather.12.cloned.1.call-start = ((), (), s32[]{:S(2)}) async-start(), calls=%async_computation.3 | async-start | bytes 3538944 | tf_op jit(solution)/shard_map/all_gather | solution.py:110
  7.3 110.6 %all-gather.8.cloned.1.call-start = ((), (), s32[]{:S(2)}) async-start(), calls=%async_computation.1 | async-start | bytes 6684672 | tf_op jit(solution)/shard_map/all_gather | solution.py:115
  8.0 149.7 %all-gather.14.cloned.1.call-start = ((), (), s32[]{:S(2)}) async-start(), calls=%async_computation.4 | async-start | bytes 4456448 | tf_op jit(solution)/shard_map/all_gather | solution.py:119
  75.4 3.5 copy-start.1
  78.8 117.8 %all-gather.16.cloned.1.call-start = ((), (), s32[]{:S(2)}) async-start(), calls=%async_computation.5 | async-start | bytes 4456448 | tf_op jit(solution)/shard_map/all_gather | solution.py:120
  80.3 564.2 %all-gather.10.cloned.1.call-start = ((), (), s32[]{:S(2)}) async-start(), calls=%async_computation.2 | async-start | bytes 3538944 | tf_op jit(solution)/shard_map/all_gather | solution.py:127
  129.1 4.3 copy-start.4
  133.4 2.9 copy-start.2
  137.4 1005.2 %all-gather.18.cloned.1.call-start = ((), (), s32[]{:S(2)}) async-start(), calls=%async_computation.7 | async-start | bytes 56623104 | tf_op jit(solution)/shard_map/all_gather | solution.py:134
  657.2 623.7 %reduce-scatter.2.cloned.1.call-start = ((), (), s32[]{:S(2)}) async-start(), calls=%async_computation.6 | async-start | bytes 7077888 | tf_op jit(solution)/shard_map/reduce_scatter | solution.py:146
Sparse Core Ops, SparseCore 0:
  9.7 65.6 all-gather.11
  77.0 40.8 all-gather.7
  119.5 38.1 all-gather.13
  159.2 37.3 all-gather.15
  198.8 62.1 all-gather.9
  657.3 485.2 all-gather.17
  1184.7 96.1 reduce-scatter.1
